TPU v7x, 32 devices: a whole 2x2x4 slice. The times are simulated.
32 devices in a mesh: groups: 2 (over y), row: 4 (over z), col: 4 (over x, core).
Axes of the slice: x: 2, y: 2, z: 4, core: 2. Of those that a mesh axis runs over, the one named last changes fastest.
Arguments:
- queries: bfloat16 [8, 512, 512], P(('groups', 'col'), 'row'), parts along dimension 0, may hold values from -6 to 6
- keys: bfloat16 [8, 512, 128], P(('groups', 'row'), 'col'), parts along dimension 0, may hold values from -6 to 6
- values: bfloat16 [8, 512, 128], P(('groups', 'row'), 'col'), parts along dimension 0, may hold values from -6 to 6
- block_list: int32 [8, 4, 4, 4], P('groups'), parts along dimension 0, may hold values from 0 to 3, as said below
- block_count: int32 [8, 4, 4], P('groups'), parts along dimension 0, may hold values from 0 to 4, as said below
Outputs:
- attended: bfloat16 [8, 512, 512], P(('groups', 'col'), 'row'), parts along dimension 0
There are 2 independent parts, one for each index of `groups`. A program takes and returns all parts, laid end to end along the dimension named above; each array names one. Nothing has to cross between parts.
Inputs may be any that keep to these rules, and one draw needn't show every extreme that they name: For query block i = c * 4 + q, the first block_count[c, q, r] entries of block_list[c, q, r] are distinct positions j in increasing order of key blocks r * 4 + j that do not lie after block i; block i itself is always listed in its panel; the remaining entries are other positions of the panel and carry no meaning. `block_count`: some query block lists all 4 blocks of some panel in every draw.
All inputs are finite; a program needn't handle non-finite values.
Results may differ from a plain program's by a relative error of at most 0.0036.
Values may be sent and summed in bfloat16 or wider, within the bound.
A program may use at most 64 MiB of HBM per device.

v0:
```python
import functools

import jax
import jax.numpy as jnp
from jax import lax
from jax.experimental import pallas as pl
from jax.experimental.pallas import tpu as pltpu
from jax.sharding import PartitionSpec as P

NEG = -1e30
LOG2E = 1.4426950408889634
CORES = 2
REACH = 2


def kernel(
    n_row, n_col, q_ref, k_ref, v_ref, list_ref, count_ref, o_ref,
    kbuf, vbuf, q_stack, acc, run_max, run_sum, lists, counts, bias,
    list_sem, recv_sem, ready, send_z, send_x, send_s,
):
    n_x = n_col // CORES
    block = k_ref.shape[1]
    head = k_ref.shape[2]
    heads = q_ref.shape[2] // head
    slots = lists.shape[1]
    z = lax.axis_index("row")
    col = lax.axis_index("col")
    x = col // CORES
    k = col % CORES
    mine = col * n_row + z
    sibling = x * CORES + (1 - k)
    factor = LOG2E / head**0.5

    def wanted(j, at_z, at_col):
        return j <= at_col * n_row + at_z

    def chip_wanted(j, at_z, at_x):
        return j <= (at_x * CORES + CORES - 1) * n_row + at_z

    def line_wanted(j, at_z):
        return j <= (n_col - 1) * n_row + at_z

    def copy(j, part, sem, row, column):
        return pltpu.make_async_remote_copy(
            src_ref=(kbuf, vbuf)[part].at[j],
            dst_ref=(kbuf, vbuf)[part].at[j],
            send_sem=sem,
            recv_sem=recv_sem.at[j, part],
            device_id={"row": row, "col": column},
            device_id_type=pl.DeviceIdType.MESH,
        )

    def arrived(j, part):
        copy(j, part, send_s.at[0, 0, 0], z, sibling).wait_recv()

    def x_copy(r, other, part):
        return copy(r * n_col + col, part, send_x.at[r, other, part], z, other * CORES + k)

    def s_copy(r, cx, part):
        return copy(r * n_col + cx * CORES + k, part, send_s.at[r, cx, part], z, sibling)

    def z_copy(r, up, hop, part):
        to = z + hop if up else z - hop
        return copy(r * n_col + col, part, send_z.at[r, up, hop - 1, part], to, col)

    def fan_out(r, parts, act):
        j = r * n_col + col
        for dx in range(1, n_x):
            other = (x + dx) % n_x

            @pl.when(chip_wanted(j, z, other))
            def _():
                for part in parts:
                    act(x_copy(r, other, part))

        @pl.when(wanted(j, z, sibling))
        def _():
            for part in parts:
                act(s_copy(r, x, part))

    def onward(r, up, parts, act, hops=(1, 2)):
        for hop in hops:
            to = z + hop if up else z - hop

            @pl.when((to >= 0) & (to < n_row) & line_wanted(r * n_col + col, to))
            def _():
                for part in parts:
                    act(z_copy(r, up, hop, part))

    def both_ways(r, parts, act):
        for up in (1, 0):
            @pl.when(((r <= z) if up else (r >= z)) & ((z - r) % REACH == 0))
            def _():
                onward(r, up, parts, act)

    def start(c):
        c.start()

    def wait_send(c):
        c.wait_send()

    list_copies = (
        pltpu.make_async_copy(list_ref.at[col, z], lists, list_sem.at[0]),
        pltpu.make_async_copy(count_ref.at[col, pl.ds(z, 1)], counts, list_sem.at[1]),
    )
    own = z * n_col + col
    own_copies = (
        pltpu.make_async_copy(k_ref.at[0], kbuf.at[own], list_sem.at[2]),
        pltpu.make_async_copy(v_ref.at[0], vbuf.at[own], list_sem.at[3]),
    )
    q_copies = [
        pltpu.make_async_copy(
            q_ref.at[0, :, pl.ds(h * head, head)], q_stack.at[pl.ds(h * block, block)], list_sem.at[4 + h]
        )
        for h in range(heads)
    ]
    for c in (*own_copies, *list_copies, *q_copies):
        c.start()

    barrier = pltpu.get_barrier_semaphore()

    def greet(row, column):
        pl.semaphore_signal(
            barrier, inc=1, device_id={"row": row, "col": column}, device_id_type=pl.DeviceIdType.MESH
        )

    greeted = jnp.int32(n_x)
    for to in (z - 1, z + 1):
        inside = (to >= 0) & (to < n_row)
        greeted += jnp.where(inside, 1, 0)

        @pl.when(inside)
        def _():
            greet(to, col)

    for dx in range(1, n_x):
        greet(z, ((x + dx) % n_x) * CORES + k)
    greet(z, sibling)
    pl.semaphore_wait(barrier, greeted)

    for c in own_copies:
        c.wait()

    @pl.when((z > 0) & (z + 1 < n_row))
    def _():
        for up, to in ((1, z - 1), (0, z + 1)):
            pl.semaphore_signal(
                ready.at[up], inc=1, device_id={"row": to, "col": col},
                device_id_type=pl.DeviceIdType.MESH,
            )

    for up in (1, 0):
        onward(z, up, (0, 1), start, (1,))
    fan_out(z, (0, 1), start)
    for up, far in ((1, z + 2), (0, z - 2)):
        @pl.when((far >= 0) & (far < n_row))
        def _():
            pl.semaphore_wait(ready.at[up], 1)
            onward(z, up, (0, 1), start, (2,))

    acc[...] = jnp.zeros_like(acc)
    run_sum[...] = jnp.zeros_like(run_sum)
    run_max[...] = jnp.full_like(run_max, NEG)
    for c in (*list_copies, *q_copies):
        c.wait()

    def fill(r, carry):
        for p in range(slots):
            hit = jnp.int32(0)
            for s in range(slots):
                hit += jnp.where((lists[r, s] == p) & (s < counts[0, r]), 1, 0)
            bias[r * slots + p] = jnp.where(hit > 0, 0.0, NEG).astype(jnp.float32)
        return carry

    lax.fori_loop(0, n_row, fill, 0)

    def attend(j, count, masked):
        rows = count * block
        key = kbuf[pl.ds(j, count)].reshape(rows, head)
        value = vbuf[pl.ds(j, count)].reshape(rows, head)
        s = lax.dot_general(
            key, q_stack[...], (((1,), (1,)), ((), ())), preferred_element_type=jnp.float32
        )
        s = jnp.concatenate(
            [s[b * block : (b + 1) * block] + bias[j + b] for b in range(count)], axis=0
        )
        if masked:
            key_row = lax.broadcasted_iota(jnp.int32, s.shape, 0)
            query_row = lax.broadcasted_iota(jnp.int32, s.shape, 1) % block
            s = jnp.where(key_row - query_row <= (mine - j) * block, s, NEG)
        old = run_max[...]
        new = jnp.maximum(old, jnp.max(s, axis=0, keepdims=True))
        w = jnp.exp2((s - new) * factor)
        decay = jnp.exp2((old - new) * factor)
        run_max[...] = new
        run_sum[...] = run_sum[...] * decay + jnp.sum(w, axis=0, keepdims=True)
        acc[...] = acc[...] * decay + lax.dot_general(
            value, w.astype(jnp.bfloat16), (((0,), (0,)), ((), ())),
            preferred_element_type=jnp.float32,
        )

    def relay_line(r):
        j = r * n_col + col

        @pl.when(line_wanted(j, z))
        def _():
            for part in range(2):
                arrived(j, part)
                both_ways(r, (part,), start)
                fan_out(r, (part,), start)

    def relay_chips(r):
        for dx in range(1, n_x):
            cx = (x + dx) % n_x
            j = r * n_col + cx * CORES + k

            @pl.when(chip_wanted(j, z, x))
            def _():
                for part in range(2):
                    arrived(j, part)

                    @pl.when(wanted(j, z, sibling))
                    def _():
                        s_copy(r, cx, part).start()

    def attend_panel(r):
        for dx in range(n_x):
            first = r * n_col + ((x + dx) % n_x) * CORES
            theirs = first + 1 - k

            @pl.when(wanted(theirs, z, col))
            def _():
                for part in range(2):
                    arrived(theirs, part)

            @pl.when(first + CORES <= mine)
            def _():
                attend(first, CORES, False)

            for c in range(CORES):
                @pl.when((first + CORES > mine) & (first + c <= mine))
                def _():
                    attend(first + c, 1, True)

    def at_distance(d, act):
        for r, first in ((z - d, True), (z + d, False)):
            @pl.when((r >= 0) & (r < n_row) & (first | (d > 0)))
            def _():
                act(r)

    relay_chips(z)
    at_distance(1, relay_line)

    def step(d, carry):
        at_distance(d, relay_line)
        at_distance(d - 1, relay_chips)
        at_distance(d - 2, attend_panel)
        return carry

    lax.fori_loop(2, n_row, step, 0)
    at_distance(n_row - 1, relay_chips)
    at_distance(n_row - 2, attend_panel)
    at_distance(n_row - 1, attend_panel)

    for h in range(heads):
        part = slice(h * block, (h + 1) * block)
        o_ref[0, :, h * head : (h + 1) * head] = (
            (acc[:, part] / run_sum[:, part]).T.astype(o_ref.dtype)
        )

    both_ways(z, (0, 1), wait_send)
    fan_out(z, (0, 1), wait_send)

    def drain(r, carry):
        @pl.when((r != z) & line_wanted(r * n_col + col, z))
        def _():
            both_ways(r, (0, 1), wait_send)
            fan_out(r, (0, 1), wait_send)

        for dx in range(1, n_x):
            cx = (x + dx) % n_x
            j = r * n_col + cx * CORES + k

            @pl.when(wanted(j, z, sibling))
            def _():
                for part in range(2):
                    s_copy(r, cx, part).wait_send()

        return carry

    lax.fori_loop(0, n_row, drain, 0)


def per_device(n_row, n_col, queries, keys, values, block_list, block_count):
    block, head = keys.shape[1], keys.shape[2]
    wide = queries.shape[1] * (queries.shape[2] // head)
    slots = block_list.shape[3]
    assert queries.shape[1] == block and slots == n_col and block_list.shape[1] == n_row
    blocks = n_row * n_col
    vmem = pl.BlockSpec(memory_space=pltpu.VMEM)
    hbm = pl.BlockSpec(memory_space=pl.ANY)
    return pl.pallas_call(
        functools.partial(kernel, n_row, n_col),
        out_shape=jax.ShapeDtypeStruct(queries.shape, queries.dtype),
        in_specs=[hbm] * 5,
        out_specs=vmem,
        scratch_shapes=[
            pltpu.VMEM((blocks, block, head), keys.dtype),
            pltpu.VMEM((blocks, block, head), values.dtype),
            pltpu.VMEM((wide, head), queries.dtype),
            pltpu.VMEM((head, wide), jnp.float32),
            pltpu.VMEM((1, wide), jnp.float32),
            pltpu.VMEM((1, wide), jnp.float32),
            pltpu.SMEM((n_row, slots), jnp.int32),
            pltpu.SMEM((1, n_row), jnp.int32),
            pltpu.SMEM((blocks,), jnp.float32),
            pltpu.SemaphoreType.DMA((4 + wide // block,)),
            pltpu.SemaphoreType.DMA((blocks, 2)),
            pltpu.SemaphoreType.REGULAR((2,)),
            pltpu.SemaphoreType.DMA((n_row, 2, REACH, 2)),
            pltpu.SemaphoreType.DMA((n_row, n_col // CORES, 2)),
            pltpu.SemaphoreType.DMA((n_row, n_col // CORES, 2)),
        ],
        compiler_params=pltpu.CompilerParams(collective_id=0, has_side_effects=True),
        name="gather_attend",
    )(queries, keys, values, block_list, block_count)


def solution(mesh):
    placed = (
        P(("groups", "col"), "row", None),
        P(("groups", "row"), "col", None),
        P(("groups", "row"), "col", None),
        P("groups", None, None, None),
        P("groups", None, None),
    )
    return jax.shard_map(
        functools.partial(per_device, mesh.shape["row"], mesh.shape["col"]),
        mesh=mesh,
        in_specs=placed,
        out_specs=P(("groups", "col"), "row", None),
        check_vma=False,
    )
```

profile of v0, /device:TPU:7, one launch (start us, length us, event | category | flops | bytes accessed | tf_op | source)
XLA Modules:
  0.0 18.5 jit_solution(5299244713217157033)
XLA Ops:
  0.0 17.0 %gather_attend.1 = bf16[1,128,512]{2,1,0:T(8,128)(2,1)} custom-call(bf16[1,128,512]{2,1,0:T(8,128)(2,1)} %q_ref.1, bf16[1,128,128]{2,1,0:T(8,128)(2,1)} %k_ref.1, bf16[1,128,128]{2,1,0:T(8,128)(2,1)} %v_ref.1, s32[4,4,4,4]{3,2,1,0:T(4,128)} %list_ref.1, s32[4,4,4]{2,1,0:T(4,128)} %count_ref.1), custom_call_target="tpu_custom_call" | custom-call | tf_op jit(solution)/shard_map/gather_attend/pallas_call | solution.py:302
  17.0 1.6 %copy.7 = bf16[1,128,512]{2,1,0:T(8,128)(2,1)} copy(bf16[1,128,512]{2,1,0:T(8,128)(2,1)} %gather_attend.1) | data formatting | bytes 262144
where the time goes:
time: 18.7 us; the launch traced here: 18.5 us
  Pallas kernels  17 us (91%)
  local copies, waits for them, and re-layouts  1.57 us (8%)
    pallas_call x1, Pallas kernels, per_device(): pl.pallas_call(functools.partial(kernel, n_row, n_col), out_shape=jax.Sha...  17 us
    unnamed x1, local copies, waits for them, and re-layouts  1.57 us

commit v1 on v0

--- a/solution.py
+++ b/solution.py
@@ -301,7 +301,7 @@
     hbm = pl.BlockSpec(memory_space=pl.ANY)
     return pl.pallas_call(
         functools.partial(kernel, n_row, n_col),
-        out_shape=jax.ShapeDtypeStruct(queries.shape, queries.dtype),
+        out_shape=pltpu.VMEM(queries.shape, queries.dtype),
         in_specs=[hbm] * 5,
         out_specs=vmem,
         scratch_shapes=[
@@ -323,7 +323,7 @@
         ],
         compiler_params=pltpu.CompilerParams(collective_id=0, has_side_effects=True),
         name="gather_attend",
-    )(queries, keys, values, block_list, block_count)
+    )(*(pltpu.with_memory_space_constraint(a, pltpu.HBM) for a in (queries, keys, values, block_list, block_count)))
 
 
 def solution(mesh):

time: 18.7 us -> 17.1 us (0.914)
  local copies, waits for them, and re-layouts: 1.57 us -> 0.66 us
  Pallas kernels: 17 us -> 16.3 us
    unnamed x1, local copies, waits for them, and re-layouts: 1.57 us -> 0.66 us
    pallas_call x1, Pallas kernels: 17 us -> 16.3 us  [per_device(): pl.pallas_call(functools.partial(kernel, n_row, n_col), out_shape=pltpu.V...]
where the time goes in v1:
time: 17.1 us; the launch traced here: 17 us
  Pallas kernels  16.3 us (95%)
  local copies, waits for them, and re-layouts  0.66 us (4%)
    pallas_call x1, Pallas kernels, per_device(): pl.pallas_call(functools.partial(kernel, n_row, n_col), out_shape=pltpu.V...  16.3 us
    unnamed x1, local copies, waits for them, and re-layouts  0.66 us

profile of v1, /device:TPU:7, one launch (start us, length us, event | category | flops | bytes accessed | tf_op | source)
XLA Modules:
  0.0 17.0 jit_solution(15364605453686127186)
XLA Ops:
  0.0 16.3 %gather_attend.1 = bf16[1,128,512]{2,1,0:T(8,128)(2,1)S(1)} custom-call(bf16[1,128,512]{2,1,0:T(8,128)(2,1)} %q_ref.1, bf16[1,128,128]{2,1,0:T(8,128)(2,1)} %k_ref.1, bf16[1,128,128]{2,1,0:T(8,128)(2,1)} %v_ref.1, s32[4,4,4,4]{3,2,1,0:T(4,128)} %list_ref.1, s32[4,4,4]{2,1,0:T(4,128)} %count_ref.1), custom_call_target="tpu_custom_call" | custom-call | tf_op jit(solution)/shard_map/gather_attend/pallas_call | solution.py:302
  16.3 0.7 %copy.7 = bf16[1,128,512]{2,1,0:T(8,128)(2,1)} copy(bf16[1,128,512]{2,1,0:T(8,128)(2,1)S(1)} %gather_attend.1) | data formatting | bytes 262144

commit v2 on v1

--- a/solution.py
+++ b/solution.py
@@ -10,13 +10,14 @@
 NEG = -1e30
 LOG2E = 1.4426950408889634
 CORES = 2
-REACH = 2
+REACH = 3
+HOPS = (1, REACH)
 
 
 def kernel(
     n_row, n_col, q_ref, k_ref, v_ref, list_ref, count_ref, o_ref,
     kbuf, vbuf, q_stack, acc, run_max, run_sum, lists, counts, bias,
-    list_sem, recv_sem, ready, send_z, send_x, send_s,
+    list_sem, recv_sem, ready_z, ready_x, send_z, send_x, send_s,
 ):
     n_x = n_col // CORES
     block = k_ref.shape[1]
@@ -54,42 +55,55 @@
         copy(j, part, send_s.at[0, 0, 0], z, sibling).wait_recv()
 
     def x_copy(r, other, part):
-        return copy(r * n_col + col, part, send_x.at[r, other, part], z, other * CORES + k)
+        j = r * n_col + col
+        same = other * CORES + k
+        to = jnp.where(wanted(j, z, same), same, other * CORES + CORES - 1)
+        return copy(j, part, send_x.at[r, other, part], z, to)
 
     def s_copy(r, cx, part):
         return copy(r * n_col + cx * CORES + k, part, send_s.at[r, cx, part], z, sibling)
 
     def z_copy(r, up, hop, part):
         to = z + hop if up else z - hop
-        return copy(r * n_col + col, part, send_z.at[r, up, hop - 1, part], to, col)
-
-    def fan_out(r, parts, act):
+        return copy(r * n_col + col, part, send_z.at[r, up, int(hop > 1), part], to, col)
+
+    def to_chips(r, parts, act, higher):
         j = r * n_col + col
         for dx in range(1, n_x):
-            other = (x + dx) % n_x
-
-            @pl.when(chip_wanted(j, z, other))
+            other = x + dx if higher else x - dx
+
+            @pl.when(((other < n_x) if higher else (other >= 0)) & chip_wanted(j, z, other))
             def _():
                 for part in parts:
                     act(x_copy(r, other, part))
 
-        @pl.when(wanted(j, z, sibling))
+    def to_sibling(r, parts, act):
+        @pl.when(wanted(r * n_col + col, z, sibling))
         def _():
             for part in parts:
                 act(s_copy(r, x, part))
 
-    def onward(r, up, parts, act, hops=(1, 2)):
+    def fan_out(r, parts, act):
+        for higher in (True, False):
+            to_chips(r, parts, act, higher)
+        to_sibling(r, parts, act)
+
+    def onward(r, up, parts, act, hops=HOPS):
         for hop in hops:
             to = z + hop if up else z - hop
-
-            @pl.when((to >= 0) & (to < n_row) & line_wanted(r * n_col + col, to))
+            gone = (z - r if up else r - z) % REACH
+
+            @pl.when(
+                (gone < (2 if hop == 1 else 1)) & (to >= 0) & (to < n_row)
+                & line_wanted(r * n_col + col, to)
+            )
             def _():
                 for part in parts:
                     act(z_copy(r, up, hop, part))
 
     def both_ways(r, parts, act):
         for up in (1, 0):
-            @pl.when(((r <= z) if up else (r >= z)) & ((z - r) % REACH == 0))
+            @pl.when((r <= z) if up else (r >= z))
             def _():
                 onward(r, up, parts, act)
 
@@ -119,44 +133,58 @@
 
     barrier = pltpu.get_barrier_semaphore()
 
-    def greet(row, column):
+    def signal(sem, row, column):
         pl.semaphore_signal(
-            barrier, inc=1, device_id={"row": row, "col": column}, device_id_type=pl.DeviceIdType.MESH
-        )
-
-    greeted = jnp.int32(n_x)
-    for to in (z - 1, z + 1):
-        inside = (to >= 0) & (to < n_row)
-        greeted += jnp.where(inside, 1, 0)
-
-        @pl.when(inside)
-        def _():
-            greet(to, col)
+            sem, inc=1, device_id={"row": row, "col": column}, device_id_type=pl.DeviceIdType.MESH
+        )
+
+    greeted = x * CORES + 1
+    for hop in HOPS:
+        greeted += jnp.where(z >= hop, 1, 0)
+
+        @pl.when(z + hop < n_row)
+        def _():
+            signal(barrier, z + hop, col)
 
     for dx in range(1, n_x):
-        greet(z, ((x + dx) % n_x) * CORES + k)
-    greet(z, sibling)
+        @pl.when(x + dx < n_x)
+        def _():
+            for c in range(CORES):
+                signal(barrier, z, (x + dx) * CORES + c)
+
+    signal(barrier, z, sibling)
     pl.semaphore_wait(barrier, greeted)
+
+    for hop in HOPS:
+        @pl.when(z >= hop)
+        def _():
+            signal(ready_z.at[int(hop > 1)], z - hop, col)
+
+    for dx in range(1, n_x):
+        @pl.when(x >= dx)
+        def _():
+            for c in range(CORES):
+                signal(ready_x.at[dx - 1], z, (x - dx) * CORES + c)
 
     for c in own_copies:
         c.wait()
 
-    @pl.when((z > 0) & (z + 1 < n_row))
-    def _():
-        for up, to in ((1, z - 1), (0, z + 1)):
-            pl.semaphore_signal(
-                ready.at[up], inc=1, device_id={"row": to, "col": col},
-                device_id_type=pl.DeviceIdType.MESH,
-            )
-
-    for up in (1, 0):
-        onward(z, up, (0, 1), start, (1,))
-    fan_out(z, (0, 1), start)
-    for up, far in ((1, z + 2), (0, z - 2)):
-        @pl.when((far >= 0) & (far < n_row))
-        def _():
-            pl.semaphore_wait(ready.at[up], 1)
-            onward(z, up, (0, 1), start, (2,))
+    onward(z, 0, (0, 1), start)
+    to_chips(z, (0, 1), start, False)
+    to_sibling(z, (0, 1), start)
+    for hop in HOPS:
+        @pl.when(z + hop < n_row)
+        def _():
+            pl.semaphore_wait(ready_z.at[int(hop > 1)], 1)
+            onward(z, 1, (0, 1), start, (hop,))
+
+        if hop == 1:
+            for dx in range(1, n_x):
+                @pl.when(x + dx < n_x)
+                def _():
+                    pl.semaphore_wait(ready_x.at[dx - 1], CORES)
+
+            to_chips(z, (0, 1), start, True)
 
     acc[...] = jnp.zeros_like(acc)
     run_sum[...] = jnp.zeros_like(run_sum)
@@ -213,8 +241,9 @@
         for dx in range(1, n_x):
             cx = (x + dx) % n_x
             j = r * n_col + cx * CORES + k
-
-            @pl.when(chip_wanted(j, z, x))
+            theirs = r * n_col + cx * CORES + 1 - k
+
+            @pl.when(wanted(j, z, col))
             def _():
                 for part in range(2):
                     arrived(j, part)
@@ -223,12 +252,20 @@
                     def _():
                         s_copy(r, cx, part).start()
 
-    def attend_panel(r):
-        for dx in range(n_x):
+            @pl.when(wanted(theirs, z, col) & jnp.logical_not(wanted(theirs, z, sibling)))
+            def _():
+                for part in range(2):
+                    arrived(theirs, part)
+
+    def attend_chips(r, dxs):
+        for dx in dxs:
             first = r * n_col + ((x + dx) % n_x) * CORES
             theirs = first + 1 - k
-
-            @pl.when(wanted(theirs, z, col))
+            passed = wanted(theirs, z, col)
+            if dx:
+                passed &= wanted(theirs, z, sibling)
+
+            @pl.when(passed)
             def _():
                 for part in range(2):
                     arrived(theirs, part)
@@ -248,19 +285,29 @@
             def _():
                 act(r)
 
+    def near(t, act):
+        d = t + jnp.where(t % REACH == 2, 1, 0) - jnp.where((t % REACH == 0) & (t > 0), 1, 0)
+        at_distance(d, act)
+
+    def attend_near(r):
+        attend_chips(r, (0,))
+
+    def attend_far(r):
+        attend_chips(r, range(1, n_x))
+
+    at_distance(1, relay_line)
     relay_chips(z)
-    at_distance(1, relay_line)
-
-    def step(d, carry):
-        at_distance(d, relay_line)
-        at_distance(d - 1, relay_chips)
-        at_distance(d - 2, attend_panel)
+    near(jnp.int32(2), relay_line)
+    attend_near(z)
+
+    def step(t, carry):
+        near(t, attend_far)
+        near(t + 3, relay_line)
+        near(t + 1, relay_chips)
+        near(t + 1, attend_near)
         return carry
 
-    lax.fori_loop(2, n_row, step, 0)
-    at_distance(n_row - 1, relay_chips)
-    at_distance(n_row - 2, attend_panel)
-    at_distance(n_row - 1, attend_panel)
+    lax.fori_loop(0, 1 - (1 - n_row) // REACH * REACH, step, 0)
 
     for h in range(heads):
         part = slice(h * block, (h + 1) * block)
@@ -281,7 +328,7 @@
             cx = (x + dx) % n_x
             j = r * n_col + cx * CORES + k
 
-            @pl.when(wanted(j, z, sibling))
+            @pl.when(wanted(j, z, sibling) & wanted(j, z, col))
             def _():
                 for part in range(2):
                     s_copy(r, cx, part).wait_send()
@@ -316,8 +363,9 @@
             pltpu.SMEM((blocks,), jnp.float32),
             pltpu.SemaphoreType.DMA((4 + wide // block,)),
             pltpu.SemaphoreType.DMA((blocks, 2)),
-            pltpu.SemaphoreType.REGULAR((2,)),
-            pltpu.SemaphoreType.DMA((n_row, 2, REACH, 2)),
+            pltpu.SemaphoreType.REGULAR((len(HOPS),)),
+            pltpu.SemaphoreType.REGULAR((max(1, n_col // CORES - 1),)),
+            pltpu.SemaphoreType.DMA((n_row, 2, len(HOPS), 2)),
             pltpu.SemaphoreType.DMA((n_row, n_col // CORES, 2)),
             pltpu.SemaphoreType.DMA((n_row, n_col // CORES, 2)),
         ],

time: 17.1 us -> 16.3 us (0.953)
  the two profiles are of different devices: /device:TPU:7 before, /device:TPU:25 now
where the time goes in v2:
time: 16.3 us; the launch traced here: 16.1 us
  Pallas kernels  15.5 us (95%)
  local copies, waits for them, and re-layouts  0.66 us (4%)
    pallas_call x1, Pallas kernels, per_device(): pl.pallas_call(functools.partial(kernel, n_row, n_col), out_shape=pltpu.V...  15.5 us
    unnamed x1, local copies, waits for them, and re-layouts  0.66 us

profile of v2, /device:TPU:25, one launch (start us, length us, event | category | flops | bytes accessed | tf_op | source)
XLA Modules:
  0.0 16.1 jit_solution(8318324466062978310)
XLA Ops:
  0.0 15.5 %gather_attend.1 = bf16[1,128,512]{2,1,0:T(8,128)(2,1)S(1)} custom-call(bf16[1,128,512]{2,1,0:T(8,128)(2,1)} %q_ref.1, bf16[1,128,128]{2,1,0:T(8,128)(2,1)} %k_ref.1, bf16[1,128,128]{2,1,0:T(8,128)(2,1)} %v_ref.1, s32[4,4,4,4]{3,2,1,0:T(4,128)} %list_ref.1, s32[4,4,4]{2,1,0:T(4,128)} %count_ref.1), custom_call_target="tpu_custom_call" | custom-call | tf_op jit(solution)/shard_map/gather_attend/pallas_call | solution.py:349
  15.5 0.7 %copy.7 = bf16[1,128,512]{2,1,0:T(8,128)(2,1)} copy(bf16[1,128,512]{2,1,0:T(8,128)(2,1)S(1)} %gather_attend.1) | data formatting | bytes 262144

commit v3 on v2

--- a/solution.py
+++ b/solution.py
@@ -275,9 +275,9 @@
                 attend(first, CORES, False)
 
             for c in range(CORES):
-                @pl.when((first + CORES > mine) & (first + c <= mine))
+                @pl.when(first + c == mine)
                 def _():
-                    attend(first + c, 1, True)
+                    attend(first, c + 1, True)
 
     def at_distance(d, act):
         for r, first in ((z - d, True), (z + d, False)):
@@ -301,10 +301,10 @@
     attend_near(z)
 
     def step(t, carry):
-        near(t, attend_far)
         near(t + 3, relay_line)
+        near(t + 1, attend_near)
         near(t + 1, relay_chips)
-        near(t + 1, attend_near)
+        near(t + 0, attend_far)
         return carry
 
     lax.fori_loop(0, 1 - (1 - n_row) // REACH * REACH, step, 0)

time: 16.3 us -> 15.3 us (0.939)
  the two profiles are of different devices: /device:TPU:25 before, /device:TPU:7 now
where the time goes in v3:
time: 15.3 us; the launch traced here: 15 us
  Pallas kernels  14.3 us (93%)
  local copies, waits for them, and re-layouts  0.66 us (4%)
    pallas_call x1, Pallas kernels, per_device(): pl.pallas_call(functools.partial(kernel, n_row, n_col), out_shape=pltpu.V...  14.3 us
    unnamed x1, local copies, waits for them, and re-layouts  0.66 us

profile of v3, /device:TPU:7, one launch (start us, length us, event | category | flops | bytes accessed | tf_op | source)
XLA Modules:
  0.0 15.0 jit_solution(16497882740818194902)
XLA Ops:
  0.0 14.3 %gather_attend.1 = bf16[1,128,512]{2,1,0:T(8,128)(2,1)S(1)} custom-call(bf16[1,128,512]{2,1,0:T(8,128)(2,1)} %q_ref.1, bf16[1,128,128]{2,1,0:T(8,128)(2,1)} %k_ref.1, bf16[1,128,128]{2,1,0:T(8,128)(2,1)} %v_ref.1, s32[4,4,4,4]{3,2,1,0:T(4,128)} %list_ref.1, s32[4,4,4]{2,1,0:T(4,128)} %count_ref.1), custom_call_target="tpu_custom_call" | custom-call | tf_op jit(solution)/shard_map/gather_attend/pallas_call | solution.py:349
  14.3 0.7 %copy.7 = bf16[1,128,512]{2,1,0:T(8,128)(2,1)} copy(bf16[1,128,512]{2,1,0:T(8,128)(2,1)S(1)} %gather_attend.1) | data formatting | bytes 262144

commit v4 on v3

--- a/solution.py
+++ b/solution.py
@@ -11,7 +11,8 @@
 LOG2E = 1.4426950408889634
 CORES = 2
 REACH = 3
-HOPS = (1, REACH)
+UP = (1, REACH)
+DOWN = (3, 1, 2)
 
 
 def kernel(
@@ -65,14 +66,14 @@
 
     def z_copy(r, up, hop, part):
         to = z + hop if up else z - hop
-        return copy(r * n_col + col, part, send_z.at[r, up, int(hop > 1), part], to, col)
-
-    def to_chips(r, parts, act, higher):
+        return copy(r * n_col + col, part, send_z.at[r, up, hop - 1, part], to, col)
+
+    def to_chips(r, parts, act, keep=lambda other: True):
         j = r * n_col + col
         for dx in range(1, n_x):
-            other = x + dx if higher else x - dx
-
-            @pl.when(((other < n_x) if higher else (other >= 0)) & chip_wanted(j, z, other))
+            other = (x + dx) % n_x
+
+            @pl.when(chip_wanted(j, z, other) & keep(other))
             def _():
                 for part in parts:
                     act(x_copy(r, other, part))
@@ -84,17 +85,16 @@
                 act(s_copy(r, x, part))
 
     def fan_out(r, parts, act):
-        for higher in (True, False):
-            to_chips(r, parts, act, higher)
+        to_chips(r, parts, act)
         to_sibling(r, parts, act)
 
-    def onward(r, up, parts, act, hops=HOPS):
-        for hop in hops:
+    def onward(r, up, parts, act, hops=None):
+        for hop in hops or (UP if up else DOWN):
             to = z + hop if up else z - hop
             gone = (z - r if up else r - z) % REACH
 
             @pl.when(
-                (gone < (2 if hop == 1 else 1)) & (to >= 0) & (to < n_row)
+                (gone < (2 if up and hop == 1 else 1)) & (to >= 0) & (to < n_row)
                 & line_wanted(r * n_col + col, to)
             )
             def _():
@@ -113,6 +113,28 @@
     def wait_send(c):
         c.wait_send()
 
+    barrier = pltpu.get_barrier_semaphore()
+
+    def signal(sem, row, column):
+        pl.semaphore_signal(
+            sem, inc=1, device_id={"row": row, "col": column}, device_id_type=pl.DeviceIdType.MESH
+        )
+
+    greeted = x * CORES + 1
+    for hop in range(1, REACH + 1):
+        greeted += jnp.where(z >= hop, 1, 0)
+
+        @pl.when(z + hop < n_row)
+        def _():
+            signal(barrier, z + hop, col)
+
+        for dx in range(1, n_x) if hop == 1 else ():
+            @pl.when(x + dx < n_x)
+            def _():
+                for c in range(CORES):
+                    signal(barrier, z, (x + dx) * CORES + c)
+
+    signal(barrier, z, sibling)
     list_copies = (
         pltpu.make_async_copy(list_ref.at[col, z], lists, list_sem.at[0]),
         pltpu.make_async_copy(count_ref.at[col, pl.ds(z, 1)], counts, list_sem.at[1]),
@@ -131,31 +153,9 @@
     for c in (*own_copies, *list_copies, *q_copies):
         c.start()
 
-    barrier = pltpu.get_barrier_semaphore()
-
-    def signal(sem, row, column):
-        pl.semaphore_signal(
-            sem, inc=1, device_id={"row": row, "col": column}, device_id_type=pl.DeviceIdType.MESH
-        )
-
-    greeted = x * CORES + 1
-    for hop in HOPS:
-        greeted += jnp.where(z >= hop, 1, 0)
-
-        @pl.when(z + hop < n_row)
-        def _():
-            signal(barrier, z + hop, col)
-
-    for dx in range(1, n_x):
-        @pl.when(x + dx < n_x)
-        def _():
-            for c in range(CORES):
-                signal(barrier, z, (x + dx) * CORES + c)
-
-    signal(barrier, z, sibling)
     pl.semaphore_wait(barrier, greeted)
 
-    for hop in HOPS:
+    for hop in UP:
         @pl.when(z >= hop)
         def _():
             signal(ready_z.at[int(hop > 1)], z - hop, col)
@@ -170,9 +170,9 @@
         c.wait()
 
     onward(z, 0, (0, 1), start)
-    to_chips(z, (0, 1), start, False)
+    to_chips(z, (0, 1), start, lambda other: other < x)
     to_sibling(z, (0, 1), start)
-    for hop in HOPS:
+    for hop in UP:
         @pl.when(z + hop < n_row)
         def _():
             pl.semaphore_wait(ready_z.at[int(hop > 1)], 1)
@@ -184,7 +184,7 @@
                 def _():
                     pl.semaphore_wait(ready_x.at[dx - 1], CORES)
 
-            to_chips(z, (0, 1), start, True)
+            to_chips(z, (0, 1), start, lambda other: other > x)
 
     acc[...] = jnp.zeros_like(acc)
     run_sum[...] = jnp.zeros_like(run_sum)
@@ -202,24 +202,27 @@
 
     lax.fori_loop(0, n_row, fill, 0)
 
-    def attend(j, count, masked):
+    def attend(j, count, masked, value_there):
         rows = count * block
         key = kbuf[pl.ds(j, count)].reshape(rows, head)
-        value = vbuf[pl.ds(j, count)].reshape(rows, head)
         s = lax.dot_general(
             key, q_stack[...], (((1,), (1,)), ((), ())), preferred_element_type=jnp.float32
-        )
-        s = jnp.concatenate(
-            [s[b * block : (b + 1) * block] + bias[j + b] for b in range(count)], axis=0
         )
         if masked:
             key_row = lax.broadcasted_iota(jnp.int32, s.shape, 0)
             query_row = lax.broadcasted_iota(jnp.int32, s.shape, 1) % block
             s = jnp.where(key_row - query_row <= (mine - j) * block, s, NEG)
         old = run_max[...]
-        new = jnp.maximum(old, jnp.max(s, axis=0, keepdims=True))
-        w = jnp.exp2((s - new) * factor)
+        parts = [s[b * block : (b + 1) * block] for b in range(count)]
+        new = old
+        for b in range(count):
+            new = jnp.maximum(new, jnp.max(parts[b], axis=0, keepdims=True) + bias[j + b])
+        w = jnp.concatenate(
+            [jnp.exp2((parts[b] - (new - 3.0 * bias[j + b])) * factor) for b in range(count)], axis=0
+        )
         decay = jnp.exp2((old - new) * factor)
+        value_there()
+        value = vbuf[pl.ds(j, count)].reshape(rows, head)
         run_max[...] = new
         run_sum[...] = run_sum[...] * decay + jnp.sum(w, axis=0, keepdims=True)
         acc[...] = acc[...] * decay + lax.dot_general(
@@ -227,115 +230,115 @@
             preferred_element_type=jnp.float32,
         )
 
-    def relay_line(r):
+    def relay_line(r, up):
         j = r * n_col + col
 
         @pl.when(line_wanted(j, z))
         def _():
             for part in range(2):
                 arrived(j, part)
-                both_ways(r, (part,), start)
+                onward(r, up, (part,), start)
                 fan_out(r, (part,), start)
 
-    def relay_chips(r):
+    def relay_chips(r, up):
         for dx in range(1, n_x):
             cx = (x + dx) % n_x
             j = r * n_col + cx * CORES + k
-            theirs = r * n_col + cx * CORES + 1 - k
-
-            @pl.when(wanted(j, z, col))
+
+            @pl.when(wanted(j, z, col) & wanted(j, z, sibling))
             def _():
                 for part in range(2):
                     arrived(j, part)
-
-                    @pl.when(wanted(j, z, sibling))
-                    def _():
-                        s_copy(r, cx, part).start()
-
-            @pl.when(wanted(theirs, z, col) & jnp.logical_not(wanted(theirs, z, sibling)))
-            def _():
-                for part in range(2):
-                    arrived(theirs, part)
+                    s_copy(r, cx, part).start()
 
     def attend_chips(r, dxs):
         for dx in dxs:
             first = r * n_col + ((x + dx) % n_x) * CORES
             theirs = first + 1 - k
-            passed = wanted(theirs, z, col)
-            if dx:
-                passed &= wanted(theirs, z, sibling)
-
-            @pl.when(passed)
-            def _():
-                for part in range(2):
+            ours = first + k
+            alone = wanted(ours, z, col) & jnp.logical_not(wanted(ours, z, sibling))
+
+            def there(part):
+                if dx:
+                    @pl.when(alone)
+                    def _():
+                        arrived(ours, part)
+
+                @pl.when(wanted(theirs, z, col))
+                def _():
                     arrived(theirs, part)
 
+            there(0)
+
             @pl.when(first + CORES <= mine)
             def _():
-                attend(first, CORES, False)
+                attend(first, CORES, False, lambda: there(1))
 
             for c in range(CORES):
                 @pl.when(first + c == mine)
                 def _():
-                    attend(first, c + 1, True)
+                    attend(first, c + 1, True, lambda: there(1))
 
     def at_distance(d, act):
-        for r, first in ((z - d, True), (z + d, False)):
-            @pl.when((r >= 0) & (r < n_row) & (first | (d > 0)))
-            def _():
-                act(r)
+        for r, up in ((z - d, 1), (z + d, 0)):
+            @pl.when((r >= 0) & (r < n_row) & ((up > 0) | (d > 0)))
+            def _():
+                act(r, up)
 
     def near(t, act):
         d = t + jnp.where(t % REACH == 2, 1, 0) - jnp.where((t % REACH == 0) & (t > 0), 1, 0)
         at_distance(d, act)
 
-    def attend_near(r):
+    def attend_near(r, up):
         attend_chips(r, (0,))
 
-    def attend_far(r):
+    def attend_far(r, up):
         attend_chips(r, range(1, n_x))
 
     at_distance(1, relay_line)
-    relay_chips(z)
+    relay_chips(z, 1)
     near(jnp.int32(2), relay_line)
-    attend_near(z)
+    attend_near(z, 1)
+
+    def settle():
+        both_ways(z, (0, 1), wait_send)
+        fan_out(z, (0, 1), wait_send)
+
+        def drain(r, carry):
+            @pl.when((r != z) & line_wanted(r * n_col + col, z))
+            def _():
+                both_ways(r, (0, 1), wait_send)
+                fan_out(r, (0, 1), wait_send)
+
+            for dx in range(1, n_x):
+                cx = (x + dx) % n_x
+                j = r * n_col + cx * CORES + k
+
+                @pl.when(wanted(j, z, sibling) & wanted(j, z, col))
+                def _():
+                    for part in range(2):
+                        s_copy(r, cx, part).wait_send()
+
+            return carry
+
+        lax.fori_loop(0, n_row, drain, 0)
+
+    last = (n_row - 1 + REACH - 1) // REACH * REACH
 
     def step(t, carry):
         near(t + 3, relay_line)
         near(t + 1, attend_near)
         near(t + 1, relay_chips)
-        near(t + 0, attend_far)
+        pl.when(t == last)(settle)
+        near(t, attend_far)
         return carry
 
-    lax.fori_loop(0, 1 - (1 - n_row) // REACH * REACH, step, 0)
-
+    lax.fori_loop(0, last + 1, step, 0)
+
+    inverse = 1.0 / run_sum[...]
     for h in range(heads):
         part = slice(h * block, (h + 1) * block)
-        o_ref[0, :, h * head : (h + 1) * head] = (
-            (acc[:, part] / run_sum[:, part]).T.astype(o_ref.dtype)
-        )
-
-    both_ways(z, (0, 1), wait_send)
-    fan_out(z, (0, 1), wait_send)
-
-    def drain(r, carry):
-        @pl.when((r != z) & line_wanted(r * n_col + col, z))
-        def _():
-            both_ways(r, (0, 1), wait_send)
-            fan_out(r, (0, 1), wait_send)
-
-        for dx in range(1, n_x):
-            cx = (x + dx) % n_x
-            j = r * n_col + cx * CORES + k
-
-            @pl.when(wanted(j, z, sibling) & wanted(j, z, col))
-            def _():
-                for part in range(2):
-                    s_copy(r, cx, part).wait_send()
-
-        return carry
-
-    lax.fori_loop(0, n_row, drain, 0)
+        o_ref[0, :, h * head : (h + 1) * head] = (acc[:, part] * inverse[:, part]).astype(o_ref.dtype).T
 
 
 def per_device(n_row, n_col, queries, keys, values, block_list, block_count):
@@ -363,9 +366,9 @@
             pltpu.SMEM((blocks,), jnp.float32),
             pltpu.SemaphoreType.DMA((4 + wide // block,)),
             pltpu.SemaphoreType.DMA((blocks, 2)),
-            pltpu.SemaphoreType.REGULAR((len(HOPS),)),
+            pltpu.SemaphoreType.REGULAR((len(UP),)),
             pltpu.SemaphoreType.REGULAR((max(1, n_col // CORES - 1),)),
-            pltpu.SemaphoreType.DMA((n_row, 2, len(HOPS), 2)),
+            pltpu.SemaphoreType.DMA((n_row, 2, REACH, 2)),
             pltpu.SemaphoreType.DMA((n_row, n_col // CORES, 2)),
             pltpu.SemaphoreType.DMA((n_row, n_col // CORES, 2)),
         ],

time: 15.3 us -> 15 us (0.980); the launches traced: 15 us -> 14.8 us
  no operation moved by 1% of the time
where the time goes in v4:
time: 15 us; the launch traced here: 14.8 us
  Pallas kernels  14.2 us (95%)
  local copies, waits for them, and re-layouts  0.66 us (4%)
    pallas_call x1, Pallas kernels, per_device(): pl.pallas_call(functools.partial(kernel, n_row, n_col), out_shape=pltpu.V...  14.2 us
    unnamed x1, local copies, waits for them, and re-layouts  0.66 us

profile of v4, /device:TPU:7, one launch (start us, length us, event | category | flops | bytes accessed | tf_op | source)
XLA Modules:
  0.0 14.8 jit_solution(3690082457464706558)
XLA Ops:
  0.0 14.2 %gather_attend.1 = bf16[1,128,512]{2,1,0:T(8,128)(2,1)S(1)} custom-call(bf16[1,128,512]{2,1,0:T(8,128)(2,1)} %q_ref.1, bf16[1,128,128]{2,1,0:T(8,128)(2,1)} %k_ref.1, bf16[1,128,128]{2,1,0:T(8,128)(2,1)} %v_ref.1, s32[4,4,4,4]{3,2,1,0:T(4,128)} %list_ref.1, s32[4,4,4]{2,1,0:T(4,128)} %count_ref.1), custom_call_target="tpu_custom_call" | custom-call | tf_op jit(solution)/shard_map/gather_attend/pallas_call | solution.py:352
  14.2 0.7 %copy.7 = bf16[1,128,512]{2,1,0:T(8,128)(2,1)} copy(bf16[1,128,512]{2,1,0:T(8,128)(2,1)S(1)} %gather_attend.1) | data formatting | bytes 262144

commit v5 on v4

--- a/solution.py
+++ b/solution.py
@@ -18,7 +18,7 @@
 def kernel(
     n_row, n_col, q_ref, k_ref, v_ref, list_ref, count_ref, o_ref,
     kbuf, vbuf, q_stack, acc, run_max, run_sum, lists, counts, bias,
-    list_sem, recv_sem, ready_z, ready_x, send_z, send_x, send_s,
+    list_sem, recv_sem, ready_z, ready_x, send_z, send_x, send_s, send_d,
 ):
     n_x = n_col // CORES
     block = k_ref.shape[1]
@@ -32,6 +32,7 @@
     mine = col * n_row + z
     sibling = x * CORES + (1 - k)
     factor = LOG2E / head**0.5
+    cross_first = n_x == 2 and n_row <= REACH + 1
 
     def wanted(j, at_z, at_col):
         return j <= at_col * n_row + at_z
@@ -41,6 +42,11 @@
 
     def line_wanted(j, at_z):
         return j <= (n_col - 1) * n_row + at_z
+
+    def on_line(j, at_z, at_x, r):
+        if not cross_first:
+            return line_wanted(j, at_z)
+        return jnp.where((r == 2) & (at_z == 0), chip_wanted(j, at_z, at_x), line_wanted(j, at_z))
 
     def copy(j, part, sem, row, column):
         return pltpu.make_async_remote_copy(
@@ -95,7 +101,7 @@
 
             @pl.when(
                 (gone < (2 if up and hop == 1 else 1)) & (to >= 0) & (to < n_row)
-                & line_wanted(r * n_col + col, to)
+                & on_line(r * n_col + col, to, x, r)
             )
             def _():
                 for part in parts:
@@ -233,19 +239,49 @@
     def relay_line(r, up):
         j = r * n_col + col
 
-        @pl.when(line_wanted(j, z))
+        @pl.when(on_line(j, z, x, r))
         def _():
             for part in range(2):
                 arrived(j, part)
                 onward(r, up, (part,), start)
                 fan_out(r, (part,), start)
 
+    def passed_down(j):
+        return (z == 2) & chip_wanted(j, 0, x) & jnp.logical_not(chip_wanted(j, 0, 1 - x))
+
+    def own_receiver(j, kc):
+        if kc == 0:
+            return jnp.where(wanted(j, z, x * CORES), 0, 1) == k
+        return k == 1
+
+    def cross_own(act_wait, act_send, act_sibling):
+        for kc in range(CORES):
+            j = z * n_col + (1 - x) * CORES + kc
+
+            @pl.when((x > 0) & passed_down(j) & own_receiver(j, kc))
+            def _():
+                for part in range(2):
+                    act_wait(j, part)
+                    act_send(copy(j, part, send_d.at[kc, part], 0, col))
+
+                    if act_sibling is not None:
+                        @pl.when((k == kc) & wanted(j, z, sibling))
+                        def _():
+                            act_sibling(s_copy(z, 1 - x, part))
+
+    def relay_own():
+        if cross_first:
+            cross_own(arrived, start, start)
+        relay_chips(z, 1)
+
     def relay_chips(r, up):
         for dx in range(1, n_x):
             cx = (x + dx) % n_x
             j = r * n_col + cx * CORES + k
 
-            @pl.when(wanted(j, z, col) & wanted(j, z, sibling))
+            later = jnp.logical_not((r == z) & (x > 0) & passed_down(j)) if cross_first else True
+
+            @pl.when(wanted(j, z, col) & wanted(j, z, sibling) & later)
             def _():
                 for part in range(2):
                     arrived(j, part)
@@ -257,6 +293,11 @@
             theirs = first + 1 - k
             ours = first + k
             alone = wanted(ours, z, col) & jnp.logical_not(wanted(ours, z, sibling))
+            sent = wanted(theirs, z, col)
+            if cross_first and dx:
+                early = (r == z) & (x > 0)
+                alone &= jnp.logical_not(early & passed_down(ours))
+                sent &= jnp.logical_not(early & passed_down(theirs) & jnp.logical_not(wanted(theirs, z, sibling)))
 
             def there(part):
                 if dx:
@@ -264,7 +305,7 @@
                     def _():
                         arrived(ours, part)
 
-                @pl.when(wanted(theirs, z, col))
+                @pl.when(sent)
                 def _():
                     arrived(theirs, part)
 
@@ -285,9 +326,9 @@
             def _():
                 act(r, up)
 
-    def near(t, act):
+    def near(t, act, swap=True):
         d = t + jnp.where(t % REACH == 2, 1, 0) - jnp.where((t % REACH == 0) & (t > 0), 1, 0)
-        at_distance(d, act)
+        at_distance(jnp.where(swap, d, t), act)
 
     def attend_near(r, up):
         attend_chips(r, (0,))
@@ -295,21 +336,30 @@
     def attend_far(r, up):
         attend_chips(r, range(1, n_x))
 
+    attend_near(z, 1)
     at_distance(1, relay_line)
-    relay_chips(z, 1)
+    relay_own()
     near(jnp.int32(2), relay_line)
-    attend_near(z, 1)
-
-    def settle():
+
+    def settle_lines():
         both_ways(z, (0, 1), wait_send)
         fan_out(z, (0, 1), wait_send)
 
         def drain(r, carry):
-            @pl.when((r != z) & line_wanted(r * n_col + col, z))
+            @pl.when((r != z) & on_line(r * n_col + col, z, x, r))
             def _():
                 both_ways(r, (0, 1), wait_send)
                 fan_out(r, (0, 1), wait_send)
 
+            return carry
+
+        lax.fori_loop(0, n_row, drain, 0)
+
+    def settle_chips():
+        if cross_first:
+            cross_own(lambda j, part: None, wait_send, None)
+
+        def drain(r, carry):
             for dx in range(1, n_x):
                 cx = (x + dx) % n_x
                 j = r * n_col + cx * CORES + k
@@ -325,12 +375,15 @@
 
     last = (n_row - 1 + REACH - 1) // REACH * REACH
 
+    paired = (x > 0) | (z < REACH)
+
     def step(t, carry):
+        near(t + 1, attend_near)
         near(t + 3, relay_line)
-        near(t + 1, attend_near)
         near(t + 1, relay_chips)
-        pl.when(t == last)(settle)
-        near(t, attend_far)
+        pl.when(t == last - 1)(settle_lines)
+        pl.when(t == last - jnp.where(paired, 0, 1))(settle_chips)
+        near(t, attend_far, paired)
         return carry
 
     lax.fori_loop(0, last + 1, step, 0)
@@ -371,6 +424,7 @@
             pltpu.SemaphoreType.DMA((n_row, 2, REACH, 2)),
             pltpu.SemaphoreType.DMA((n_row, n_col // CORES, 2)),
             pltpu.SemaphoreType.DMA((n_row, n_col // CORES, 2)),
+            pltpu.SemaphoreType.DMA((CORES, 2)),
         ],
         compiler_params=pltpu.CompilerParams(collective_id=0, has_side_effects=True),
         name="gather_attend",

time: 15 us -> 14.7 us (0.980)
  the two profiles are of different devices: /device:TPU:7 before, /device:TPU:17 now
where the time goes in v5:
time: 14.7 us; the launch traced here: 14.5 us
  Pallas kernels  13.8 us (94%)
  local copies, waits for them, and re-layouts  0.66 us (4%)
    pallas_call x1, Pallas kernels, per_device(): pl.pallas_call(functools.partial(kernel, n_row, n_col), out_shape=pltpu.V...  13.8 us
    unnamed x1, local copies, waits for them, and re-layouts  0.66 us

profile of v5, /device:TPU:17, one launch (start us, length us, event | category | flops | bytes accessed | tf_op | source)
XLA Modules:
  0.0 14.5 jit_solution(1885690577739229305)
XLA Ops:
  0.0 13.8 %gather_attend.1 = bf16[1,128,512]{2,1,0:T(8,128)(2,1)S(1)} custom-call(bf16[1,128,512]{2,1,0:T(8,128)(2,1)} %q_ref.1, bf16[1,128,128]{2,1,0:T(8,128)(2,1)} %k_ref.1, bf16[1,128,128]{2,1,0:T(8,128)(2,1)} %v_ref.1, s32[4,4,4,4]{3,2,1,0:T(4,128)} %list_ref.1, s32[4,4,4]{2,1,0:T(4,128)} %count_ref.1), custom_call_target="tpu_custom_call" | custom-call | tf_op jit(solution)/shard_map/gather_attend/pallas_call | solution.py:405
  13.8 0.7 %copy.7 = bf16[1,128,512]{2,1,0:T(8,128)(2,1)} copy(bf16[1,128,512]{2,1,0:T(8,128)(2,1)S(1)} %gather_attend.1) | data formatting | bytes 262144

commit v6 on v5

--- a/solution.py
+++ b/solution.py
@@ -18,7 +18,7 @@
 def kernel(
     n_row, n_col, q_ref, k_ref, v_ref, list_ref, count_ref, o_ref,
     kbuf, vbuf, q_stack, acc, run_max, run_sum, lists, counts, bias,
-    list_sem, recv_sem, ready_z, ready_x, send_z, send_x, send_s, send_d,
+    list_sem, recv_sem, ready_z, ready_x, ready_d, send_z, send_x, send_s, send_d, send_e,
 ):
     n_x = n_col // CORES
     block = k_ref.shape[1]
@@ -79,7 +79,9 @@
         for dx in range(1, n_x):
             other = (x + dx) % n_x
 
-            @pl.when(chip_wanted(j, z, other) & keep(other))
+            ahead = (r == 0) & (z == 2) & (x > 0) if cross_first else False
+
+            @pl.when(chip_wanted(j, z, other) & keep(other) & jnp.logical_not(ahead))
             def _():
                 for part in parts:
                     act(x_copy(r, other, part))
@@ -191,6 +193,17 @@
                     pl.semaphore_wait(ready_x.at[dx - 1], CORES)
 
             to_chips(z, (0, 1), start, lambda other: other > x)
+            if cross_first:
+                @pl.when((z == 1) & (z + 1 < n_row))
+                def _():
+                    @pl.when(x == 0)
+                    def _():
+                        for c in range(CORES):
+                            signal(ready_d, z, CORES + c)
+
+                    @pl.when(x > 0)
+                    def _():
+                        pl.semaphore_wait(ready_d, CORES)
 
     acc[...] = jnp.zeros_like(acc)
     run_sum[...] = jnp.zeros_like(run_sum)
@@ -236,6 +249,14 @@
             preferred_element_type=jnp.float32,
         )
 
+    def ahead_copies(r, part, act):
+        j = r * n_col + col
+
+        @pl.when((r == 0) & (z == 1) & (z + 1 < n_row) & (x > 0) & chip_wanted(j, z + 1, 0))
+        def _():
+            to = jnp.where(wanted(j, z + 1, k), k, CORES - 1)
+            act(copy(j, part, send_e.at[part], z + 1, to))
+
     def relay_line(r, up):
         j = r * n_col + col
 
@@ -245,6 +266,10 @@
                 arrived(j, part)
                 onward(r, up, (part,), start)
                 fan_out(r, (part,), start)
+
+            if cross_first and up:
+                for part in range(2):
+                    ahead_copies(r, part, start)
 
     def passed_down(j):
         return (z == 2) & chip_wanted(j, 0, x) & jnp.logical_not(chip_wanted(j, 0, 1 - x))
@@ -342,6 +367,10 @@
     near(jnp.int32(2), relay_line)
 
     def settle_lines():
+        if cross_first:
+            for part in range(2):
+                ahead_copies(0, part, wait_send)
+
         both_ways(z, (0, 1), wait_send)
         fan_out(z, (0, 1), wait_send)
 
@@ -380,13 +409,13 @@
     def step(t, carry):
         near(t + 1, attend_near)
         near(t + 3, relay_line)
+        pl.when(t == last - 2)(settle_lines)
         near(t + 1, relay_chips)
-        pl.when(t == last - 1)(settle_lines)
-        pl.when(t == last - jnp.where(paired, 0, 1))(settle_chips)
         near(t, attend_far, paired)
         return carry
 
     lax.fori_loop(0, last + 1, step, 0)
+    settle_chips()
 
     inverse = 1.0 / run_sum[...]
     for h in range(heads):
@@ -421,10 +450,12 @@
             pltpu.SemaphoreType.DMA((blocks, 2)),
             pltpu.SemaphoreType.REGULAR((len(UP),)),
             pltpu.SemaphoreType.REGULAR((max(1, n_col // CORES - 1),)),
+            pltpu.SemaphoreType.REGULAR,
             pltpu.SemaphoreType.DMA((n_row, 2, REACH, 2)),
             pltpu.SemaphoreType.DMA((n_row, n_col // CORES, 2)),
             pltpu.SemaphoreType.DMA((n_row, n_col // CORES, 2)),
             pltpu.SemaphoreType.DMA((CORES, 2)),
+            pltpu.SemaphoreType.DMA((2,)),
         ],
         compiler_params=pltpu.CompilerParams(collective_id=0, has_side_effects=True),
         name="gather_attend",

time: 14.7 us -> 14.6 us (level)
  the two profiles are of different devices: /device:TPU:17 before, /device:TPU:18 now
where the time goes in v6:
time: 14.6 us; the launch traced here: 14.4 us
  Pallas kernels  13.7 us (94%)
  local copies, waits for them, and re-layouts  0.66 us (5%)
    pallas_call x1, Pallas kernels, per_device(): pl.pallas_call(functools.partial(kernel, n_row, n_col), out_shape=pltpu.V...  13.7 us
    unnamed x1, local copies, waits for them, and re-layouts  0.66 us

profile of v6, /device:TPU:18, one launch (start us, length us, event | category | flops | bytes accessed | tf_op | source)
XLA Modules:
  0.0 14.4 jit_solution(9066803122312355205)
XLA Ops:
  0.0 13.7 %gather_attend.1 = bf16[1,128,512]{2,1,0:T(8,128)(2,1)S(1)} custom-call(bf16[1,128,512]{2,1,0:T(8,128)(2,1)} %q_ref.1, bf16[1,128,128]{2,1,0:T(8,128)(2,1)} %k_ref.1, bf16[1,128,128]{2,1,0:T(8,128)(2,1)} %v_ref.1, s32[4,4,4,4]{3,2,1,0:T(4,128)} %list_ref.1, s32[4,4,4]{2,1,0:T(4,128)} %count_ref.1), custom_call_target="tpu_custom_call" | custom-call | tf_op jit(solution)/shard_map/gather_attend/pallas_call | solution.py:434
  13.7 0.7 %copy.7 = bf16[1,128,512]{2,1,0:T(8,128)(2,1)} copy(bf16[1,128,512]{2,1,0:T(8,128)(2,1)S(1)} %gather_attend.1) | data formatting | bytes 262144

commit v7 on v6

--- a/solution.py
+++ b/solution.py
@@ -32,7 +32,8 @@
     mine = col * n_row + z
     sibling = x * CORES + (1 - k)
     factor = LOG2E / head**0.5
-    cross_first = n_x == 2 and n_row <= REACH + 1
+    short = n_row <= REACH + 1
+    cross_first = n_x == 2 and short
 
     def wanted(j, at_z, at_col):
         return j <= at_col * n_row + at_z
@@ -264,7 +265,8 @@
         def _():
             for part in range(2):
                 arrived(j, part)
-                onward(r, up, (part,), start)
+                if up or not short:
+                    onward(r, up, (part,), start, (1,) if short else None)
                 fan_out(r, (part,), start)
 
             if cross_first and up:
@@ -377,7 +379,12 @@
         def drain(r, carry):
             @pl.when((r != z) & on_line(r * n_col + col, z, x, r))
             def _():
-                both_ways(r, (0, 1), wait_send)
+                if short:
+                    @pl.when(r < z)
+                    def _():
+                        onward(r, 1, (0, 1), wait_send, (1,))
+                else:
+                    both_ways(r, (0, 1), wait_send)
                 fan_out(r, (0, 1), wait_send)
 
             return carry
@@ -405,12 +412,14 @@
     last = (n_row - 1 + REACH - 1) // REACH * REACH
 
     paired = (x > 0) | (z < REACH)
+    late = (x > 0) & (z == 2) & (k == 0)
 
     def step(t, carry):
-        near(t + 1, attend_near)
+        near(jnp.where(late, n_row + REACH, t + 1), attend_near)
         near(t + 3, relay_line)
         pl.when(t == last - 2)(settle_lines)
         near(t + 1, relay_chips)
+        near(jnp.where(late, t + 1, n_row + REACH), attend_near)
         near(t, attend_far, paired)
         return carry
 

time: 14.6 us -> 14.6 us (level)
  the two profiles are of different devices: /device:TPU:18 before, /device:TPU:27 now
where the time goes in v7:
time: 14.6 us; the launch traced here: 14.4 us
  Pallas kernels  13.7 us (94%)
  local copies, waits for them, and re-layouts  0.66 us (5%)
    pallas_call x1, Pallas kernels, per_device(): pl.pallas_call(functools.partial(kernel, n_row, n_col), out_shape=pltpu.V...  13.7 us
    unnamed x1, local copies, waits for them, and re-layouts  0.66 us

profile of v7, /device:TPU:27, one launch (start us, length us, event | category | flops | bytes accessed | tf_op | source)
XLA Modules:
  0.0 14.4 jit_solution(7495857965664870693)
XLA Ops:
  0.0 13.7 %gather_attend.1 = bf16[1,128,512]{2,1,0:T(8,128)(2,1)S(1)} custom-call(bf16[1,128,512]{2,1,0:T(8,128)(2,1)} %q_ref.1, bf16[1,128,128]{2,1,0:T(8,128)(2,1)} %k_ref.1, bf16[1,128,128]{2,1,0:T(8,128)(2,1)} %v_ref.1, s32[4,4,4,4]{3,2,1,0:T(4,128)} %list_ref.1, s32[4,4,4]{2,1,0:T(4,128)} %count_ref.1), custom_call_target="tpu_custom_call" | custom-call | tf_op jit(solution)/shard_map/gather_attend/pallas_call | solution.py:443
  13.8 0.7 %copy.7 = bf16[1,128,512]{2,1,0:T(8,128)(2,1)} copy(bf16[1,128,512]{2,1,0:T(8,128)(2,1)S(1)} %gather_attend.1) | data formatting | bytes 262144
